TPU v7x, 32 devices: a whole 2x2x4 slice. The times are simulated.
32 devices in a mesh: cols: 2 (over core), space: 16 (over z, y, x).
Axes of the slice: x: 2, y: 2, z: 4, core: 2. Of those that a mesh axis runs over, the one named last changes fastest.
Arguments:
- mean_state: float32 [6, 256, 256], P(None, 'space', 'cols'), may hold values from -2 to 2
- covariance: float32 [128, 6, 256, 256], P('cols', None, 'space'), may hold values from -2 to 2
- land_mask: int32 [256, 256], replicated, may hold values 0 or 1
- stations: int32 [2048], P('space'), may hold values from 0 to 65535, as said below
- observed: float32 [2048], P('space'), may hold values from -5 to 5
- obs_weight: float32 [2048], P('space'), may hold values from 0.5 to 4
Outputs:
- mean_analysis: float32 [6, 256, 256], P(None, 'space', 'cols')
- covariance_analysis: float32 [128, 6, 256, 256], P('cols', None, 'space')
Inputs may be any that keep to these rules, and one draw needn't show every extreme that they name: Stations b * 128 to (b + 1) * 128 - 1 lie in grid rows b * 16 to (b + 1) * 16 - 1; several stations may share a cell.
All inputs are finite; a program needn't handle non-finite values.
Results may differ from a plain program's by a relative error of at most 0.0053.
Values may be sent and summed in bfloat16 or wider, within the bound.
No kernel may reach another device: no remote copies, remote signals or barrier semaphores. Data moves between devices by JAX's collectives and lax.ppermute only.
A program may use at most 128 MiB of HBM per device.

v0:
```python
import jax
import jax.numpy as jnp
from jax import lax
from jax.sharding import PartitionSpec as P

ITERS = 4
time_step = 0.5
gravity = 1.0
reduced_gravity = 0.125
coriolis = 0.3
friction = 0.05
layer_depths = (1.0, 2.0)


def padded_2(block, sides, width):
    for axis, dim in sides:
        count = lax.axis_size(axis)
        forward = [(i, i + 1) for i in range(count - 1)]
        backward = [(target, source) for source, target in forward]
        low = lax.ppermute(
            lax.slice_in_dim(block, block.shape[dim] - width, None, axis=dim), axis, forward
        )
        high = lax.ppermute(lax.slice_in_dim(block, 0, width, axis=dim), axis, backward)
        block = jnp.concatenate([low, block, high], axis=dim)
    return block


def diff_rows(values):
    return 0.5 * (values[..., 2:, 1:-1] - values[..., :-2, 1:-1])


def diff_cols(values):
    return 0.5 * (values[..., 1:-1, 2:] - values[..., 1:-1, :-2])


def inner(values):
    return values[..., 1:-1, 1:-1]


def velocities(field, wet_cells):
    wet_inner = inner(wet_cells)
    surface = field[..., 0, :, :] + field[..., 3, :, :]
    pressure_top = gravity * surface
    pressure_pair = (pressure_top, pressure_top - reduced_gravity * field[..., 0, :, :])
    velocity_pairs = []
    for layer_index in range(2):
        zonal = inner(field[..., 3 * layer_index + 1, :, :])
        north = inner(field[..., 3 * layer_index + 2, :, :])
        pressure = pressure_pair[layer_index]
        zonal_new = wet_inner * (
            zonal + time_step * (-diff_rows(pressure) + coriolis * north - friction * zonal)
        )
        north_new = wet_inner * (
            north + time_step * (-diff_cols(pressure) - coriolis * zonal - friction * north)
        )
        velocity_pairs.append((zonal_new, north_new))
    return velocity_pairs


def mean_core(padded, wet_cells):
    velocity_pairs = velocities(padded, wet_cells)
    fields = []
    carried = []
    for layer_index in range(2):
        thickness = padded[3 * layer_index]
        column_depth = layer_depths[layer_index] + inner(thickness)
        zonal_new, north_new = velocity_pairs[layer_index]
        updated = thickness[2:-2, 2:-2] - time_step * (
            diff_rows(column_depth * zonal_new) + diff_cols(column_depth * north_new)
        )
        fields += [updated, zonal_new[1:-1, 1:-1], north_new[1:-1, 1:-1]]
        carried += [thickness[1:-1, 2:-2], zonal_new[:, 1:-1], north_new[:, 1:-1]]
    return (jnp.stack(fields), jnp.stack(carried))


def tangent_core(padded, carried, wet_cells):
    beside_all = jnp.pad(carried, ((0, 0), (0, 0), (1, 1)))
    velocity_pairs = velocities(padded, wet_cells)
    fields = []
    for layer_index in range(2):
        thickness = padded[..., 3 * layer_index, :, :]
        column_depth = layer_depths[layer_index] + beside_all[3 * layer_index]
        zonal_new, north_new = velocity_pairs[layer_index]
        flux_rows = column_depth * zonal_new + inner(thickness) * beside_all[3 * layer_index + 1]
        flux_cols = column_depth * north_new + inner(thickness) * beside_all[3 * layer_index + 2]
        updated = thickness[..., 2:-2, 2:-2] - time_step * (
            diff_rows(flux_rows) + diff_cols(flux_cols)
        )
        fields += [updated, zonal_new[..., 1:-1, 1:-1], north_new[..., 1:-1, 1:-1]]
    return jnp.stack(fields, axis=-3)


def local(mean_state, covariance, land_mask, stations, observed, obs_weight):
    local_cols = covariance.shape[0]
    tile_rows = covariance.shape[2]
    grid_cols = covariance.shape[3]
    piece_cols = mean_state.shape[2]
    total_cols = local_cols * lax.axis_size("cols")
    space_index = lax.axis_index("space")
    column_index = lax.axis_index("cols")
    land_float = land_mask.astype(jnp.float32)
    first_row = space_index * tile_rows
    columns = covariance
    depth = 2 * ITERS
    grid_rows = tile_rows * lax.axis_size("space")
    mean_now = lax.all_gather(mean_state, "cols", axis=2, tiled=True)
    mean_now = padded_2(mean_now, (("space", 1),), depth)
    columns = padded_2(columns, (("space", 2),), depth)
    wet_deep = jnp.pad(land_float, ((depth, depth), (2, 2)))
    rows_here = first_row - depth + jnp.arange(tile_rows + 2 * depth, dtype=jnp.int32)
    inside = jnp.logical_and(rows_here >= 0, rows_here < grid_rows).astype(jnp.float32)
    for step_index in range(ITERS):
        extent = depth - 2 * step_index
        shrink = 2 * step_index
        wet_cells = lax.dynamic_slice_in_dim(
            wet_deep, first_row + shrink, tile_rows + 2 * extent, 0
        )
        padded_mean = jnp.pad(mean_now, ((0, 0), (0, 0), (2, 2)))
        mean_next, carried = mean_core(padded_mean, wet_cells)
        padded_columns = jnp.pad(columns, ((0, 0), (0, 0), (0, 0), (2, 2)))
        columns_next = tangent_core(padded_columns, carried, wet_cells)
        keep = inside[shrink + 2 : shrink + 2 + tile_rows + 2 * (extent - 2)]
        mean_now = mean_next * keep[None, :, None]
        columns = columns_next * keep[:, None]
    mean_piece = lax.dynamic_slice_in_dim(mean_now, column_index * piece_cols, piece_cols, 2)
    surface = mean_now[0] + mean_now[3]
    offset_stations = stations - first_row * grid_cols
    column_surface = (columns[:, 0] + columns[:, 3]).reshape(local_cols, tile_rows * grid_cols)
    sensed_local = jnp.take(column_surface, offset_stations, axis=1) * obs_weight[None, :]
    innovation = obs_weight * (observed - jnp.take(surface.reshape(-1), offset_stations))
    sensed = lax.all_gather(sensed_local, "cols", axis=0, tiled=True)
    products = jnp.dot(
        sensed, sensed.T, precision=lax.Precision.HIGHEST, preferred_element_type=jnp.float32
    )
    target_part = jnp.dot(
        sensed, innovation, precision=lax.Precision.HIGHEST, preferred_element_type=jnp.float32
    )
    gram_sum, target = lax.psum((products, target_part), "space")
    identity = jnp.eye(total_cols, dtype=jnp.float32)
    gram_matrix = identity + gram_sum
    lower_factor = lax.linalg.cholesky(gram_matrix)
    halfway = lax.linalg.triangular_solve(lower_factor, target[:, None], left_side=True, lower=True)
    weights = lax.linalg.triangular_solve(
        lower_factor, halfway, left_side=True, lower=True, transpose_a=True
    )[:, 0]
    inverse = lax.linalg.triangular_solve(lower_factor, identity, left_side=True, lower=True)
    transform_low = inverse.T.astype(jnp.bfloat16)
    weights_local = lax.dynamic_slice_in_dim(weights, column_index * local_cols, local_cols)
    increment_terms = jnp.einsum(
        "k,kfrc->frc", weights_local, columns, precision=lax.Precision.HIGHEST
    )
    increment_total = lax.psum(increment_terms, "cols")
    increment = lax.dynamic_slice_in_dim(increment_total, column_index * piece_cols, piece_cols, 2)
    columns_low = columns.astype(jnp.bfloat16)
    shard_piece = lax.all_gather(columns_low, "cols", axis=0, tiled=True)
    transform_part = lax.dynamic_slice(
        transform_low, (0, column_index * local_cols), (shard_piece.shape[0], local_cols)
    )
    updated = jnp.einsum(
        "kj,kfrc->jfrc", transform_part, shard_piece, preferred_element_type=jnp.float32
    )
    return (mean_piece + increment, updated)


def solution(mesh):
    return jax.shard_map(
        local,
        mesh=mesh,
        in_specs=(
            P(None, "space", "cols"),
            P("cols", None, "space", None),
            P(),
            P("space"),
            P("space"),
            P("space"),
        ),
        out_specs=(P(None, "space", "cols"), P("cols", None, "space", None)),
        check_vma=False,
    )
```

profile of v0, /device:TPU:0, one launch (start us, length us, event | category | flops | bytes accessed | tf_op | source)
XLA Modules:
  0.0 518.4 jit_solution(15029220077060353122)
XLA Ops:
  7.2 6.4 %copy.20 = f32[64,6,16,256]{3,0,2,1:T(8,128)S(1)} copy(f32[64,6,16,256]{3,2,1,0:T(8,128)} %param.7) | data formatting | bytes 12582912 | tf_op args[1]
  18.5 7.3 %collective-permute-start.2 = (f32[64,6,8,256]{3,0,2,1:T(8,128)S(1)}, f32[64,6,8,256]{3,0,2,1:T(8,128)}, u32[]{:S(2)}, u32[]{:S(2)}) collective-permute-start(f32[64,6,8,256]{3,0,2,1:T(8,128)S(1)} %get-tuple-element.128), channel_id=1, source_target_pairs={{0,1},{1,2},{2,3},{3,4},{4,5},{5,6},{6,7},{7,8},{8,9},{9,10},{10,1... | collective-permute-start | bytes 9437192 | tf_op jit(solution)/shard_map/ppermute | solution.py:20
  29.6 5.2 collective-permute-start
  39.9 119.6 %collective-permute-done.1 = f32[6,8,256]{2,1,0:T(8,128)} collective-permute-done((f32[6,8,256]{2,1,0:T(8,128)}, f32[6,8,256]{2,1,0:T(8,128)}, u32[]{:S(2)}, u32[]{:S(2)}) %collective-permute-start.1) | collective-permute-done | bytes 49184 | tf_op jit(solution)/shard_map/ppermute | solution.py:23
  181.5 9.8 %select_maximum_fusion = f32[64,6,32,260]{3,0,2,1:T(8,128)S(1)} fusion(f32[64,6,8,256]{3,0,2,1:T(8,128)} %collective-permute-done.3, f32[64,6,16,256]{3,0,2,1:T(8,128)} %copy-done, f32[64,6,8,256]{3,0,2,1:T(8,128)} %collective-permute-done.2), kind=kLoop, calls=%fused_computation.16 | loop fusion | flops 25559040 | bytes 25362432 | tf_op jit(solution)/shard_map/concatenate | solution.py:24
  191.4 6.6 %slice_bitcast_fusion = (f32[64,32,260]{2,0,1:T(8,128)}, f32[64,32,260]{2,0,1:T(8,128)}, f32[64,32,260]{2,0,1:T(8,128)}, f32[64,32,260]{2,0,1:T(8,128)}, f32[64,32,260]{2,0,1:T(8,128)}, /*index=5*/f32[64,32,260]{2,0,1:T(8,128)}) fusion(f32[64,6,32,260]{3,0,2,1:T(8,128)S(1)} %select_maximum_fusion), kind=kLoop, calls=%fused_computation.28 | loop fusion | bytes 25559040 | tf_op jit(solution)/shard_map/squeeze | solution.py:48
  200.3 12.8 %multiply_add_fusion.3 = (f32[64,30,258]{2,0,1:T(8,128)S(1)}, f32[64,30,258]{2,0,1:T(8,128)}, f32[64,30,258]{2,0,1:T(8,128)S(1)}, f32[64,30,258]{2,0,1:T(8,128)S(1)}) fusion(f32[64,32,260]{2,0,1:T(8,128)} %get-tuple-element.85, f32[30,258]{1,0:T(8,128)S(1)} %copy-done.51, f32[30,258]{1,0:T(8,128)S(1)} %copy-done.53, f32[64,32,260]{2,0,1:T(8,128)} %get-tuple-element.82, ...), kind=kLoop, calls=%fused_computation.71 | loop fusion | flops 12879360 | bytes 21919680 | tf_op jit(solution)/shard_map/add | solution.py:84
  213.2 3.2 fusion.116
  220.9 6.3 %multiply_add_fusion.1 = (f32[64,30,258]{2,0,1:T(8,128)S(1)}, f32[64,30,258]{2,0,1:T(8,128)}, f32[64,30,258]{2,0,1:T(8,128)S(1)}, f32[64,30,258]{2,0,1:T(8,128)S(1)}) fusion(f32[64,32,260]{2,0,1:T(8,128)S(1)} %copy-done.2, f32[30,258]{1,0:T(8,128)S(1)} %copy-done.48, f32[30,258]{1,0:T(8,128)S(1)} %copy-done.49, f32[64,32,260]{2,0,1:T(8,128)S(1)} %copy-done.4, ...), kind=kLoop, calls=%fused_computation.69 | loop fusion | flops 12879360 | bytes 21919680 | tf_op jit(solution)/shard_map/add | solution.py:84
  227.2 3.3 fusion.109
  234.0 6.5 %broadcast_multiply_fusion = f32[64,6,28,256]{3,0,2,1:T(8,128)S(1)} fusion(f32[64,6,28,256]{3,0,2,1:T(8,128)} %fusion.103, f32[28]{0:T(128)S(1)} %copy-done.73), kind=kLoop, calls=%fused_computation.25 | loop fusion | flops 2752512 | bytes 22020208 | tf_op jit(solution)/shard_map/mul | solution.py:124
  240.5 6.7 %fusion.34 = (f32[64,28,260]{2,0,1:T(8,128)}, f32[64,28,260]{2,0,1:T(8,128)}, f32[64,28,260]{2,0,1:T(8,128)S(1)}, f32[64,28,260]{2,0,1:T(8,128)}, f32[64,28,260]{2,0,1:T(8,128)}, /*index=5*/f32[64,28,260]{2,0,1:T(8,128)S(1)}) fusion(f32[64,6,28,256]{3,0,2,1:T(8,128)S(1)} %broadcast_multiply_fusion), kind=kLoop, calls=%fused_computation.77 | loop fusion | bytes 22192128 | tf_op jit(solution)/shard_map/squeeze | solution.py:48
  247.3 2.9 multiply_subtract_fusion.1
  250.2 8.1 %multiply_add_fusion.7 = (f32[64,26,258]{2,0,1:T(8,128)S(1)}, f32[64,26,258]{2,0,1:T(8,128)}, f32[64,26,258]{2,0,1:T(8,128)S(1)}, f32[64,26,258]{2,0,1:T(8,128)}) fusion(f32[64,28,260]{2,0,1:T(8,128)S(1)} %get-tuple-element.101, f32[26,258]{1,0:T(8,128)S(1)} %copy-done.45, f32[26,258]{1,0:T(8,128)S(1)} %copy-done.47, f32[64,28,260]{2,0,1:T(8,128)} %get-tuple-element.99, ...), kind=kLoop, calls=%fused_computation.114 | loop fusion | flops 11162112 | bytes 18997056 | tf_op jit(solution)/shard_map/add | solution.py:84
  262.8 5.8 %multiply_add_fusion.5 = (f32[64,26,258]{2,0,1:T(8,128)S(1)}, f32[64,26,258]{2,0,1:T(8,128)}, f32[64,26,258]{2,0,1:T(8,128)S(1)}, f32[64,26,258]{2,0,1:T(8,128)}) fusion(f32[64,28,260]{2,0,1:T(8,128)S(1)} %get-tuple-element.98, f32[26,258]{1,0:T(8,128)S(1)} %get-tuple-element.142, f32[26,258]{1,0:T(8,128)S(1)} %get-tuple-element.145, ...), kind=kLoop, calls=%fused_computation.112 | loop fusion | flops 11162112 | bytes 18997056 | tf_op jit(solution)/shard_map/add | solution.py:84
  274.6 4.0 fusion.68
  281.2 5.8 %multiply_add_fusion.11 = (f32[64,22,258]{2,0,1:T(8,128)S(1)}, f32[64,22,258]{2,0,1:T(8,128)}, f32[64,22,258]{2,0,1:T(8,128)S(1)}, f32[64,22,258]{2,0,1:T(8,128)}) fusion(f32[64,24,260]{2,0,1:T(8,128)S(1)} %get-tuple-element.113, f32[22,258]{1,0:T(8,128)S(1)} %copy-done.57, f32[22,258]{1,0:T(8,128)} %get-tuple-element.185, ...), kind=kLoop, calls=%fused_computation.157 | loop fusion | flops 9444864 | bytes 16074432 | tf_op jit(solution)/shard_map/add | solution.py:84
  290.5 3.9 multiply_add_fusion.9
  297.9 7.0 %fusion.102 = (f32[64,20,260]{2,0,1:T(8,128)}, f32[64,20,260]{2,0,1:T(8,128)}, f32[64,20,260]{2,0,1:T(8,128)S(1)}, f32[64,20,260]{2,0,1:T(8,128)}, f32[64,20,260]{2,0,1:T(8,128)}, /*index=5*/f32[64,20,260]{2,0,1:T(8,128)}) fusion(f32[64,6,20,256]{3,0,2,1:T(8,128)S(1)} %broadcast_multiply_fusion.2), kind=kLoop, calls=%fused_computation.163 | loop fusion | bytes 15851520 | tf_op jit(solution)/shard_map/squeeze | solution.py:48
  307.6 3.0 multiply_add_fusion.15
  314.1 3.5 multiply_add_fusion.13
  319.4 3.2 fusion.427
  322.7 2.7 copy-done.1
  330.2 41.4 %psum.22 = f32[128]{0:T(128)S(1)} all-reduce(f32[128]{0:T(128)S(1)} %convolution_bitcast_fusion.2), channel_id=1, replica_groups=mesh['cols'=2,'space'=16] {'space'}, use_global_device_ids=true, to_apply=%region_3.4 | all-reduce | flops 128 | bytes 1024 | tf_op jit(solution)/shard_map/psum | solution.py:138
  371.6 62.5 %all-reduce.16.cloned.1.call-done = f32[128,128]{1,0:T(8,128)} async-done(((f32[128,128]{1,0:T(8,128)}), f32[128,128]{1,0:T(8,128)}) %all-reduce.16.cloned.1.call-update) | async-done | bytes 65552 | tf_op jit(solution)/shard_map/psum | solution.py:138
  435.9 11.7 %cholesky.18 = f32[128,128]{1,0:T(8,128)S(1)} custom-call(f32[128,128]{1,0:T(8,128)S(1)} %fusion.193), custom_call_target="Cholesky" | custom-call | tf_op jit(solution)/shard_map/cholesky | solution.py:141
  449.0 9.8 %custom-call.9 = f32[1,128,128]{1,2,0:T(8,128)S(1)} custom-call(f32[1,128,128]{2,1,0:T(8,128)S(1)} %fusion.188), custom_call_target="InvertDiagBlocksLowerTriangular" | custom-call | tf_op jit(solution)/shard_map/triangular_solve | solution.py:143
  459.1 5.1 fusion.409
  465.9 16.0 %all-reduce.18.cloned.1.call-done = f32[6,16,256]{2,1,0:T(8,128)} async-done(((f32[6,16,256]{2,1,0:T(8,128)}), f32[6,16,256]{2,1,0:T(8,128)}) %all-reduce.18.cloned.1.call-update) | async-done | bytes 98320 | tf_op jit(solution)/shard_map/psum | solution.py:152
  483.4 18.1 %all-gather.2.cloned.1.call-done = bf16[128,6,16,256]{3,0,2,1:T(8,128)(2,1)} async-done(((bf16[64,6,16,256]{3,0,2,1:T(8,128)(2,1)}), bf16[128,6,16,256]{3,0,2,1:T(8,128)(2,1)}) %all-gather.2.cloned.1.call-update) | async-done | bytes 6291472 | tf_op jit(solution)/shard_map/all_gather | solution.py:155
  501.5 3.8 fusion.397
  505.3 6.3 %copy.27 = f32[64,6,16,256]{3,2,1,0:T(8,128)} copy(f32[64,6,16,256]{3,0,2,1:T(8,128)S(1)} %fusion.397) | data formatting | bytes 12582912
  (305 shorter events, 84.9 us)
Async XLA Ops:
  7.2 426.9 %all-reduce.16.cloned.1.call-start = ((), (), s32[]{:S(2)}) async-start(), calls=%async_computation | async-start | bytes 131072 | tf_op jit(solution)/shard_map/psum | solution.py:138
  13.6 3.7 copy-start
  13.6 12.2 %copy-start.65 = (f32[6,16,128]{2,1,0:T(8,128)S(1)}, f32[6,16,128]{2,1,0:T(8,128)}, u32[]{:S(2)}) copy-start(f32[6,16,128]{2,1,0:T(8,128)} %param.6) | copy-start | bytes 147460
  13.6 21.1 %copy-start.80 = (s32[128]{0:T(128)S(1)}, s32[128]{0:T(128)}, u32[]{:S(2)}) copy-start(s32[128]{0:T(128)} %param.9) | copy-start | bytes 1540
  17.2 164.3 %collective-permute-start.3 = (f32[64,6,8,256]{3,0,2,1:T(8,128)}, f32[64,6,8,256]{3,0,2,1:T(8,128)}, u32[]{:S(2)}, u32[]{:S(2)}) collective-permute-start(f32[64,6,8,256]{3,0,2,1:T(8,128)} %get-tuple-element.129), channel_id=1, source_target_pairs={{1,0},{2,1},{3,2},{4,3},{5,4},{6,5},{7,6},{8,7},{9,8},{10,9},{11,1... | collective-permute-start | bytes 9437192 | tf_op jit(solution)/shard_map/ppermute | solution.py:23
  18.5 163.0 %collective-permute-start.2 = (f32[64,6,8,256]{3,0,2,1:T(8,128)S(1)}, f32[64,6,8,256]{3,0,2,1:T(8,128)}, u32[]{:S(2)}, u32[]{:S(2)}) collective-permute-start(f32[64,6,8,256]{3,0,2,1:T(8,128)S(1)} %get-tuple-element.128), channel_id=1, source_target_pairs={{0,1},{1,2},{2,3},{3,4},{4,5},{5,6},{6,7},{7,8},{8,9},{9,10},{10,1... | collective-permute-start | bytes 9437192 | tf_op jit(solution)/shard_map/ppermute | solution.py:20
  28.3 131.2 %collective-permute-start.1 = (f32[6,8,256]{2,1,0:T(8,128)}, f32[6,8,256]{2,1,0:T(8,128)}, u32[]{:S(2)}, u32[]{:S(2)}) collective-permute-start(f32[6,8,256]{2,1,0:T(8,128)} %get-tuple-element.195), channel_id=1, source_target_pairs={{1,0},{2,1},{3,2},{4,3},{5,4},{6,5},{7,6},{8,7},{9,8},{10,9},{11,1... | collective-permute-start | bytes 147464 | tf_op jit(solution)/shard_map/ppermute | solution.py:23
  29.6 131.3 %collective-permute-start = (f32[6,8,256]{2,1,0:T(8,128)S(1)}, f32[6,8,256]{2,1,0:T(8,128)}, u32[]{:S(2)}, u32[]{:S(2)}) collective-permute-start(f32[6,8,256]{2,1,0:T(8,128)S(1)} %get-tuple-element.194), channel_id=1, source_target_pairs={{0,1},{1,2},{2,3},{3,4},{4,5},{5,6},{6,7},{7,8},{8,9},{9,10},{10,1... | collective-permute-start | bytes 147464 | tf_op jit(solution)/shard_map/ppermute | solution.py:20
  39.9 123.0 %copy-start.72 = (f32[28]{0:T(128)S(1)}, f32[28]{0:T(128)}, u32[]{:S(2)}) copy-start(f32[28]{0:T(128)} %slice.1097) | copy-start | bytes 340
  163.7 3.0 copy-start.36
  163.7 3.0 copy-start.38
  163.7 3.0 copy-start.40
  164.4 3.1 copy-start.68
  166.5 12.2 %copy-start.29 = (f32[28,260]{1,0:T(8,128)S(1)}, f32[28,260]{1,0:T(8,128)}, u32[]{:S(2)}) copy-start(f32[28,260]{1,0:T(8,128)} %copy-done.28) | copy-start | bytes 87364
  166.7 12.9 %copy-start.39 = (f32[26,258]{1,0:T(8,128)S(1)}, f32[26,258]{1,0:T(8,128)}, u32[]{:S(2)}) copy-start(f32[26,258]{1,0:T(8,128)} %copy-done.38) | copy-start | bytes 80500
  166.7 13.9 %copy-start.37 = (f32[26,258]{1,0:T(8,128)S(1)}, f32[26,258]{1,0:T(8,128)}, u32[]{:S(2)}) copy-start(f32[26,258]{1,0:T(8,128)} %copy-done.36) | copy-start | bytes 80500
  167.7 13.9 %copy-start.30 = (f32[6,16,256]{2,1,0:T(8,128)}, f32[6,16,256]{2,1,0:T(8,128)S(1)}, u32[]{:S(2)}) copy-start(f32[6,16,256]{2,1,0:T(8,128)S(1)} %broadcast_multiply_fusion.7) | copy-start | bytes 294916
  200.3 12.8 %copy-start.3 = (f32[64,32,260]{2,0,1:T(8,128)S(1)}, f32[64,32,260]{2,0,1:T(8,128)}, u32[]{:S(2)}) copy-start(f32[64,32,260]{2,0,1:T(8,128)} %get-tuple-element.85) | copy-start | bytes 6389764
  213.1 3.2 copy-start.10
  213.1 6.8 %copy-start.5 = (f32[64,32,260]{2,0,1:T(8,128)S(1)}, f32[64,32,260]{2,0,1:T(8,128)}, u32[]{:S(2)}) copy-start(f32[64,32,260]{2,0,1:T(8,128)} %get-tuple-element.81) | copy-start | bytes 6389764
  216.3 3.6 copy-start.4
  227.2 3.3 copy-start.9
  247.3 2.9 copy-start.45
  247.3 2.9 copy-start.46
  247.3 2.9 copy-start.47
  260.1 2.7 copy-start.8
  325.5 4.4 copy-start.67
  325.5 4.4 copy-start.78
  325.5 4.4 copy-start.79
  329.9 152.1 %all-reduce.18.cloned.1.call-start = ((), (), s32[]{:S(2)}) async-start(), calls=%async_computation.1 | async-start | bytes 196608 | tf_op jit(solution)/shard_map/psum | solution.py:152
  464.3 17.7 %copy-start.31 = (f32[6,16,256]{2,1,0:T(8,128)S(1)}, f32[6,16,256]{2,1,0:T(8,128)}, u32[]{:S(2)}) copy-start(f32[6,16,256]{2,1,0:T(8,128)} %copy-done.30) | copy-start | bytes 294916
  464.9 36.6 %all-gather.2.cloned.1.call-start = ((), (), s32[]{:S(2)}) async-start(), calls=%async_computation.2 | async-start | bytes 9437184 | tf_op jit(solution)/shard_map/all_gather | solution.py:155
  (56 other events, 115.9 us)
Sparse Core Ops, SparseCore 0:
  330.0 104.0 all-reduce.15
  465.1 16.8 all-reduce.17
  483.5 17.9 all-gather.1
where the time goes:
time: 526 us; the launch traced here: 518 us
  waiting for transfers between devices  218 us (41%)
  other arithmetic  134 us (25%)
  local copies, waits for them, and re-layouts  80.1 us (15%)
  blocking collectives  45.1 us (9%)
  starting transfers between devices  15.3 us (3%)
  between operations  15.2 us (3%)
  matrix products  10.6 us (2%)
    ppermute x2, waiting for transfers between devices, padded_2(): lax.ppermute(lax.slice_in_dim(block, 0, width, axis=dim), axis, backward)  120 us
    psum x1, waiting for transfers between devices, local(): gram_sum, target = lax.psum((products, target_part), 'space')  62.5 us
    add x8, other arithmetic, tangent_core(): column_depth * zonal_new  49.2 us
    psum x1, blocking collectives, local(): gram_sum, target = lax.psum((products, target_part), 'space')  41.4 us
    unnamed x209, local copies, waits for them, and re-layouts  41.1 us
    squeeze x4, local copies, waits for them, and re-layouts, velocities(): north = inner(field[..., 3 * layer_index + 2, :, :])  24.3 us
    all_gather x1, waiting for transfers between devices, local(): shard_piece = lax.all_gather(columns_low, 'cols', axis=0, tiled=True)  18.1 us
    psum x1, waiting for transfers between devices, local(): increment_total = lax.psum(increment_terms, 'cols')  16 us
  transfers between devices with their start and end apart: 7, of which 5 were waited for; matrix products, arithmetic and copies ran while one was open for 5% of the time, Pallas kernels for 0%

commit v1 on v0

--- a/solution.py
+++ b/solution.py
@@ -149,7 +149,8 @@
     increment_terms = jnp.einsum(
         "k,kfrc->frc", weights_local, columns, precision=lax.Precision.HIGHEST
     )
-    increment_total = lax.psum(increment_terms, "cols")
+    parts = lax.all_gather(increment_terms, "cols", axis=0, tiled=False)
+    increment_total = parts.sum(axis=0)
     increment = lax.dynamic_slice_in_dim(increment_total, column_index * piece_cols, piece_cols, 2)
     columns_low = columns.astype(jnp.bfloat16)
     shard_piece = lax.all_gather(columns_low, "cols", axis=0, tiled=True)

time: 526 us -> 484 us (0.920)
  waiting for transfers between devices: 218 us -> 177 us
    all_gather x1, waiting for transfers between devices: 18.1 us -> 0.03 us  [local(): shard_piece = lax.all_gather(columns_low, 'cols', axis=0, tiled=True)]
    psum x1 -> x0, waiting for transfers between devices: 16 us -> none  [local(): increment_total = lax.psum(increment_terms, 'cols')]
    psum x1, waiting for transfers between devices: 62.5 us -> 55.5 us  [local(): gram_sum, target = lax.psum((products, target_part), 'space')]
    unnamed x209 -> x187, local copies, waits for them, and re-layouts: 41.1 us -> 38.1 us
    unnamed x17 -> x18, other arithmetic: 16 us -> 17.5 us
  transfers between devices with their start and end apart: 7 -> 6, of which waited for: 5 -> 3; matrix products, arithmetic and copies ran while one was open for 5% -> 11% of each run, Pallas kernels for 0% -> 0%
where the time goes in v1:
time: 484 us; the launch traced here: 477 us
  waiting for transfers between devices  177 us (37%)
  other arithmetic  134 us (28%)
  local copies, waits for them, and re-layouts  75.7 us (16%)
  blocking collectives  47.3 us (10%)
  between operations  16.7 us (3%)
  starting transfers between devices  15.1 us (3%)
  matrix products  10.6 us (2%)
    ppermute x2, waiting for transfers between devices, padded_2(): lax.ppermute(lax.slice_in_dim(block, 0, width, axis=dim), axis, backward)  120 us
    psum x1, waiting for transfers between devices, local(): gram_sum, target = lax.psum((products, target_part), 'space')  55.5 us
    add x8, other arithmetic, tangent_core(): column_depth * zonal_new  49.2 us
    psum x1, blocking collectives, local(): gram_sum, target = lax.psum((products, target_part), 'space')  41.4 us
    unnamed x187, local copies, waits for them, and re-layouts  38.1 us
    squeeze x4, local copies, waits for them, and re-layouts, velocities(): north = inner(field[..., 3 * layer_index + 2, :, :])  24.3 us
    unnamed x18, other arithmetic  17.5 us
    ppermute x2, starting transfers between devices, padded_2(): lax.ppermute(lax.slice_in_dim(block, block.shape[dim] - width, None, axis...  12.4 us
  transfers between devices with their start and end apart: 6, of which 3 were waited for; matrix products, arithmetic and copies ran while one was open for 11% of the time, Pallas kernels for 0%

profile of v1, /device:TPU:0, one launch (start us, length us, event | category | flops | bytes accessed | tf_op | source)
XLA Modules:
  0.0 476.5 jit_solution(11927369375241534054)
XLA Ops:
  8.0 6.4 %copy.20 = f32[64,6,16,256]{3,0,2,1:T(8,128)S(1)} copy(f32[64,6,16,256]{3,2,1,0:T(8,128)} %param.7) | data formatting | bytes 12582912 | tf_op args[1]
  14.4 2.6 fusion.460
  19.3 7.3 %collective-permute-start.2 = (f32[64,6,8,256]{3,0,2,1:T(8,128)S(1)}, f32[64,6,8,256]{3,0,2,1:T(8,128)}, u32[]{:S(2)}, u32[]{:S(2)}) collective-permute-start(f32[64,6,8,256]{3,0,2,1:T(8,128)S(1)} %get-tuple-element.128), channel_id=1, source_target_pairs={{0,1},{1,2},{2,3},{3,4},{4,5},{5,6},{6,7},{7,8},{8,9},{9,10},{10,1... | collective-permute-start | bytes 9437192 | tf_op jit(solution)/shard_map/ppermute | solution.py:20
  30.4 5.2 %collective-permute-start = (f32[6,8,256]{2,1,0:T(8,128)S(1)}, f32[6,8,256]{2,1,0:T(8,128)}, u32[]{:S(2)}, u32[]{:S(2)}) collective-permute-start(f32[6,8,256]{2,1,0:T(8,128)S(1)} %get-tuple-element.194), channel_id=1, source_target_pairs={{0,1},{1,2},{2,3},{3,4},{4,5},{5,6},{6,7},{7,8},{8,9},{9,10},{10,1... | collective-permute-start | bytes 147464 | tf_op jit(solution)/shard_map/ppermute | solution.py:20
  40.6 119.7 %collective-permute-done.1 = f32[6,8,256]{2,1,0:T(8,128)} collective-permute-done((f32[6,8,256]{2,1,0:T(8,128)}, f32[6,8,256]{2,1,0:T(8,128)}, u32[]{:S(2)}, u32[]{:S(2)}) %collective-permute-start.1) | collective-permute-done | bytes 49184 | tf_op jit(solution)/shard_map/ppermute | solution.py:23
  173.4 9.2 %select_maximum_fusion = f32[64,6,32,260]{3,0,2,1:T(8,128)S(1)} fusion(f32[64,6,8,256]{3,0,2,1:T(8,128)} %collective-permute-done.3, f32[64,6,16,256]{3,0,2,1:T(8,128)S(1)} %bitcast.549, f32[64,6,8,256]{3,0,2,1:T(8,128)} %collective-permute-done.2), kind=kLoop, calls=%fused_computation.16 | loop fusion | flops 25559040 | bytes 25362432 | tf_op jit(solution)/shard_map/concatenate | solution.py:24
  182.6 6.6 %slice_bitcast_fusion = (f32[64,32,260]{2,0,1:T(8,128)}, f32[64,32,260]{2,0,1:T(8,128)}, f32[64,32,260]{2,0,1:T(8,128)}, f32[64,32,260]{2,0,1:T(8,128)}, f32[64,32,260]{2,0,1:T(8,128)}, /*index=5*/f32[64,32,260]{2,0,1:T(8,128)}) fusion(f32[64,6,32,260]{3,0,2,1:T(8,128)S(1)} %select_maximum_fusion), kind=kLoop, calls=%fused_computation.28 | loop fusion | bytes 25559040 | tf_op jit(solution)/shard_map/squeeze | solution.py:48
  191.5 12.9 %multiply_add_fusion.3 = (f32[64,30,258]{2,0,1:T(8,128)S(1)}, f32[64,30,258]{2,0,1:T(8,128)}, f32[64,30,258]{2,0,1:T(8,128)S(1)}, f32[64,30,258]{2,0,1:T(8,128)S(1)}) fusion(f32[64,32,260]{2,0,1:T(8,128)} %get-tuple-element.85, f32[30,258]{1,0:T(8,128)S(1)} %copy-done.34, f32[30,258]{1,0:T(8,128)S(1)} %copy-done.36, f32[64,32,260]{2,0,1:T(8,128)} %get-tuple-element.82, ...), kind=kLoop, calls=%fused_computation.71 | loop fusion | flops 12879360 | bytes 21919680 | tf_op jit(solution)/shard_map/add | solution.py:84
  204.4 3.2 fusion.116
  212.1 6.3 %multiply_add_fusion.1 = (f32[64,30,258]{2,0,1:T(8,128)S(1)}, f32[64,30,258]{2,0,1:T(8,128)}, f32[64,30,258]{2,0,1:T(8,128)S(1)}, f32[64,30,258]{2,0,1:T(8,128)S(1)}) fusion(f32[64,32,260]{2,0,1:T(8,128)S(1)} %copy-done.2, f32[30,258]{1,0:T(8,128)S(1)} %copy-done.31, f32[30,258]{1,0:T(8,128)S(1)} %copy-done.32, f32[64,32,260]{2,0,1:T(8,128)S(1)} %copy-done.4, ...), kind=kLoop, calls=%fused_computation.69 | loop fusion | flops 12879360 | bytes 21919680 | tf_op jit(solution)/shard_map/add | solution.py:84
  218.4 3.3 fusion.109
  225.3 6.5 %broadcast_multiply_fusion = f32[64,6,28,256]{3,0,2,1:T(8,128)S(1)} fusion(f32[64,6,28,256]{3,0,2,1:T(8,128)} %fusion.103, f32[28]{0:T(128)S(1)} %copy-done.62), kind=kLoop, calls=%fused_computation.25 | loop fusion | flops 2752512 | bytes 22020208 | tf_op jit(solution)/shard_map/mul | solution.py:124
  231.8 6.7 %fusion.34 = (f32[64,28,260]{2,0,1:T(8,128)}, f32[64,28,260]{2,0,1:T(8,128)}, f32[64,28,260]{2,0,1:T(8,128)S(1)}, f32[64,28,260]{2,0,1:T(8,128)}, f32[64,28,260]{2,0,1:T(8,128)}, /*index=5*/f32[64,28,260]{2,0,1:T(8,128)S(1)}) fusion(f32[64,6,28,256]{3,0,2,1:T(8,128)S(1)} %broadcast_multiply_fusion), kind=kLoop, calls=%fused_computation.77 | loop fusion | bytes 22192128 | tf_op jit(solution)/shard_map/squeeze | solution.py:48
  238.5 2.9 multiply_subtract_fusion.1
  241.5 8.1 %multiply_add_fusion.7 = (f32[64,26,258]{2,0,1:T(8,128)S(1)}, f32[64,26,258]{2,0,1:T(8,128)}, f32[64,26,258]{2,0,1:T(8,128)S(1)}, f32[64,26,258]{2,0,1:T(8,128)}) fusion(f32[64,28,260]{2,0,1:T(8,128)S(1)} %get-tuple-element.101, f32[26,258]{1,0:T(8,128)S(1)} %copy-done.28, f32[26,258]{1,0:T(8,128)S(1)} %copy-done.30, f32[64,28,260]{2,0,1:T(8,128)} %get-tuple-element.99, ...), kind=kLoop, calls=%fused_computation.114 | loop fusion | flops 11162112 | bytes 18997056 | tf_op jit(solution)/shard_map/add | solution.py:84
  254.1 5.8 %multiply_add_fusion.5 = (f32[64,26,258]{2,0,1:T(8,128)S(1)}, f32[64,26,258]{2,0,1:T(8,128)}, f32[64,26,258]{2,0,1:T(8,128)S(1)}, f32[64,26,258]{2,0,1:T(8,128)}) fusion(f32[64,28,260]{2,0,1:T(8,128)S(1)} %get-tuple-element.98, f32[26,258]{1,0:T(8,128)S(1)} %copy-done.25, f32[26,258]{1,0:T(8,128)S(1)} %copy-done.26, f32[64,28,260]{2,0,1:T(8,128)S(1)} %copy-done.7, ...), kind=kLoop, calls=%fused_computation.112 | loop fusion | flops 11162112 | bytes 18997056 | tf_op jit(solution)/shard_map/add | solution.py:84
  265.9 4.0 fusion.68
  269.9 2.5 multiply_subtract_fusion.2
  272.4 5.8 %multiply_add_fusion.11 = (f32[64,22,258]{2,0,1:T(8,128)S(1)}, f32[64,22,258]{2,0,1:T(8,128)}, f32[64,22,258]{2,0,1:T(8,128)S(1)}, f32[64,22,258]{2,0,1:T(8,128)}) fusion(f32[64,24,260]{2,0,1:T(8,128)S(1)} %get-tuple-element.113, f32[22,258]{1,0:T(8,128)S(1)} %copy-done.44, f32[22,258]{1,0:T(8,128)} %get-tuple-element.185, ...), kind=kLoop, calls=%fused_computation.157 | loop fusion | flops 9444864 | bytes 16074432 | tf_op jit(solution)/shard_map/add | solution.py:84
  281.8 3.9 multiply_add_fusion.9
  289.2 7.0 %fusion.102 = (f32[64,20,260]{2,0,1:T(8,128)}, f32[64,20,260]{2,0,1:T(8,128)}, f32[64,20,260]{2,0,1:T(8,128)S(1)}, f32[64,20,260]{2,0,1:T(8,128)}, f32[64,20,260]{2,0,1:T(8,128)}, /*index=5*/f32[64,20,260]{2,0,1:T(8,128)}) fusion(f32[64,6,20,256]{3,0,2,1:T(8,128)S(1)} %broadcast_multiply_fusion.2), kind=kLoop, calls=%fused_computation.163 | loop fusion | bytes 15851520 | tf_op jit(solution)/shard_map/squeeze | solution.py:48
  298.9 3.0 multiply_add_fusion.15
  305.3 3.5 multiply_add_fusion.13
  310.7 3.2 fusion.427
  313.9 2.7 copy-done.1
  328.6 41.4 %psum.15 = f32[128]{0:T(128)S(1)} all-reduce(f32[128]{0:T(128)S(1)} %convolution_bitcast_fusion.2), channel_id=1, replica_groups=mesh['cols'=2,'space'=16] {'space'}, use_global_device_ids=true, to_apply=%region_3.4 | all-reduce | flops 128 | bytes 1024 | tf_op jit(solution)/shard_map/psum | solution.py:138
  370.0 55.5 %all-reduce.15.cloned.1.call-done = f32[128,128]{1,0:T(8,128)} async-done(((f32[128,128]{1,0:T(8,128)}), f32[128,128]{1,0:T(8,128)}) %all-reduce.15.cloned.1.call-update) | async-done | bytes 65552 | tf_op jit(solution)/shard_map/psum | solution.py:138
  427.3 11.7 %cholesky.18 = f32[128,128]{1,0:T(8,128)S(1)} custom-call(f32[128,128]{1,0:T(8,128)S(1)} %fusion.193), custom_call_target="Cholesky" | custom-call | tf_op jit(solution)/shard_map/cholesky | solution.py:141
  440.4 9.8 %custom-call.9 = f32[1,128,128]{1,2,0:T(8,128)S(1)} custom-call(f32[1,128,128]{2,1,0:T(8,128)S(1)} %fusion.188), custom_call_target="InvertDiagBlocksLowerTriangular" | custom-call | tf_op jit(solution)/shard_map/triangular_solve | solution.py:143
  450.5 5.1 %fusion.409 = f32[1,6,16,256]{3,0,2,1:T(1,128)S(1)} fusion(f32[64,6,16,256]{3,0,2,1:T(8,128)} %copy-done.1, f32[128]{0:T(128)S(1)} %convolution_bitcast_fusion, s32[]{:T(128)S(6)} %select_n.47), kind=kOutput, calls=%fused_computation.722 | convolution fusion | flops 18874368 | bytes 6390276 | tf_op jit(solution)/shard_map/k,kfrc->frc/dot_general | solution.py:149
  458.8 3.8 fusion.397
  462.5 6.3 %copy.27 = f32[64,6,16,256]{3,2,1,0:T(8,128)} copy(f32[64,6,16,256]{3,0,2,1:T(8,128)S(1)} %fusion.397) | data formatting | bytes 12582912
  (283 shorter events, 77.9 us)
Async XLA Ops:
  8.0 417.5 %all-reduce.15.cloned.1.call-start = ((), (), s32[]{:S(2)}) async-start(), calls=%async_computation | async-start | bytes 131072 | tf_op jit(solution)/shard_map/psum | solution.py:138
  14.4 3.7 copy-start
  14.4 12.2 %copy-start.56 = (f32[6,16,128]{2,1,0:T(8,128)S(1)}, f32[6,16,128]{2,1,0:T(8,128)}, u32[]{:S(2)}) copy-start(f32[6,16,128]{2,1,0:T(8,128)} %param.6) | copy-start | bytes 147460
  14.4 21.1 %copy-start.67 = (s32[128]{0:T(128)S(1)}, s32[128]{0:T(128)}, u32[]{:S(2)}) copy-start(s32[128]{0:T(128)} %param.9) | copy-start | bytes 1540
  18.1 155.3 %collective-permute-start.3 = (f32[64,6,8,256]{3,0,2,1:T(8,128)}, f32[64,6,8,256]{3,0,2,1:T(8,128)}, u32[]{:S(2)}, u32[]{:S(2)}) collective-permute-start(f32[64,6,8,256]{3,0,2,1:T(8,128)} %get-tuple-element.129), channel_id=1, source_target_pairs={{1,0},{2,1},{3,2},{4,3},{5,4},{6,5},{7,6},{8,7},{9,8},{10,9},{11,1... | collective-permute-start | bytes 9437192 | tf_op jit(solution)/shard_map/ppermute | solution.py:23
  19.3 154.0 %collective-permute-start.2 = (f32[64,6,8,256]{3,0,2,1:T(8,128)S(1)}, f32[64,6,8,256]{3,0,2,1:T(8,128)}, u32[]{:S(2)}, u32[]{:S(2)}) collective-permute-start(f32[64,6,8,256]{3,0,2,1:T(8,128)S(1)} %get-tuple-element.128), channel_id=1, source_target_pairs={{0,1},{1,2},{2,3},{3,4},{4,5},{5,6},{6,7},{7,8},{8,9},{9,10},{10,1... | collective-permute-start | bytes 9437192 | tf_op jit(solution)/shard_map/ppermute | solution.py:20
  29.1 131.2 %collective-permute-start.1 = (f32[6,8,256]{2,1,0:T(8,128)}, f32[6,8,256]{2,1,0:T(8,128)}, u32[]{:S(2)}, u32[]{:S(2)}) collective-permute-start(f32[6,8,256]{2,1,0:T(8,128)} %get-tuple-element.195), channel_id=1, source_target_pairs={{1,0},{2,1},{3,2},{4,3},{5,4},{6,5},{7,6},{8,7},{9,8},{10,9},{11,1... | collective-permute-start | bytes 147464 | tf_op jit(solution)/shard_map/ppermute | solution.py:23
  30.4 131.3 %collective-permute-start = (f32[6,8,256]{2,1,0:T(8,128)S(1)}, f32[6,8,256]{2,1,0:T(8,128)}, u32[]{:S(2)}, u32[]{:S(2)}) collective-permute-start(f32[6,8,256]{2,1,0:T(8,128)S(1)} %get-tuple-element.194), channel_id=1, source_target_pairs={{0,1},{1,2},{2,3},{3,4},{4,5},{5,6},{6,7},{7,8},{8,9},{9,10},{10,1... | collective-permute-start | bytes 147464 | tf_op jit(solution)/shard_map/ppermute | solution.py:20
  40.6 123.2 %copy-start.61 = (f32[28]{0:T(128)S(1)}, f32[28]{0:T(128)}, u32[]{:S(2)}) copy-start(f32[28]{0:T(128)} %slice.1097) | copy-start | bytes 340
  161.7 11.7 %slice-start = ((s8[6291456]{0:T(1024)(128)(4,1)}), s8[4194304]{0:T(1024)(128)(4,1)S(1)}, s32[]{:S(2)}) async-start(s8[6291456]{0:T(1024)(128)(4,1)} %bitcast.548), calls=%async_computation.2 | async-start | bytes 8388608
  165.2 8.3 %slice-start.1 = ((s8[6291456]{0:T(1024)(128)(4,1)}), s8[2097152]{0:T(1024)(128)(4,1)S(1)}, s32[]{:S(2)}) async-start(s8[6291456]{0:T(1024)(128)(4,1)} %bitcast.548), calls=%async_computation.3 | async-start | bytes 4194304
  166.5 6.8 %copy-start.21 = (f32[20,260]{1,0:T(8,128)}, f32[20,260]{1,0:T(8,128)S(1)}, u32[]{:S(2)}) copy-start(f32[20,260]{1,0:T(8,128)S(1)} %get-tuple-element.173) | copy-start | bytes 62404
  166.5 6.8 %copy-start.24 = (f32[20,260]{1,0:T(8,128)}, f32[20,260]{1,0:T(8,128)S(1)}, u32[]{:S(2)}) copy-start(f32[20,260]{1,0:T(8,128)S(1)} %get-tuple-element.177) | copy-start | bytes 62404
  167.9 5.5 %copy-start.22 = (f32[18,258]{1,0:T(8,128)}, f32[18,258]{1,0:T(8,128)S(1)}, u32[]{:S(2)}) copy-start(f32[18,258]{1,0:T(8,128)S(1)} %get-tuple-element.12) | copy-start | bytes 55732
  167.9 5.5 %copy-start.37 = (f32[18,258]{1,0:T(8,128)}, f32[18,258]{1,0:T(8,128)S(1)}, u32[]{:S(2)}) copy-start(f32[18,258]{1,0:T(8,128)S(1)} %get-tuple-element.11) | copy-start | bytes 55732
  168.7 4.7 copy-start.38
  168.7 4.7 copy-start.39
  168.7 4.7 copy-start.40
  191.5 12.9 %copy-start.3 = (f32[64,32,260]{2,0,1:T(8,128)S(1)}, f32[64,32,260]{2,0,1:T(8,128)}, u32[]{:S(2)}) copy-start(f32[64,32,260]{2,0,1:T(8,128)} %get-tuple-element.85) | copy-start | bytes 6389764
  204.4 3.2 copy-start.10
  204.4 6.8 %copy-start.5 = (f32[64,32,260]{2,0,1:T(8,128)S(1)}, f32[64,32,260]{2,0,1:T(8,128)}, u32[]{:S(2)}) copy-start(f32[64,32,260]{2,0,1:T(8,128)} %get-tuple-element.81) | copy-start | bytes 6389764
  207.6 3.6 copy-start.4
  218.4 3.3 copy-start.9
  238.5 2.9 copy-start.29
  238.5 2.9 copy-start.30
  317.4 4.5 copy-start.54
  317.4 4.5 copy-start.55
  317.4 7.0 %copy-start.52 = (f32[18,258]{1,0:T(8,128)S(1)}, f32[18,258]{1,0:T(8,128)}, u32[]{:S(2)}) copy-start(f32[18,258]{1,0:T(8,128)} %get-tuple-element.10) | copy-start | bytes 55732
  317.4 7.0 %copy-start.53 = (f32[18,258]{1,0:T(8,128)S(1)}, f32[18,258]{1,0:T(8,128)}, u32[]{:S(2)}) copy-start(f32[18,258]{1,0:T(8,128)} %get-tuple-element.13) | copy-start | bytes 55732
  317.4 11.0 %copy-start.58 = (s32[128]{0:T(128)S(1)}, s32[128]{0:T(128)}, u32[]{:S(2)}) copy-start(s32[128]{0:T(128)} %copy-done.57) | copy-start | bytes 1540
  317.5 11.0 %copy-start.66 = (f32[128]{0:T(128)S(1)}, f32[128]{0:T(128)}, u32[]{:S(2)}) copy-start(f32[128]{0:T(128)} %param.10) | copy-start | bytes 1540
  321.3 137.4 %all-gather.3.cloned.1.call-start = ((), (), s32[]{:S(2)}) async-start(), calls=%async_computation.1 | async-start | bytes 9437184 | tf_op jit(solution)/shard_map/all_gather | solution.py:156
  (44 other events, 96.7 us)
Sparse Core Ops, SparseCore 0:
  321.4 104.0 all-reduce.14
Sparse Core Ops, SparseCore 1:
  323.3 17.2 all-gather.2
